TPU v7x, 512 devices: a whole 4x4x16 slice. The times are simulated.
512 devices in a mesh: atoms: 16 (over z), pivots: 32 (over y, x, core).
Axes of the slice: x: 4, y: 4, z: 16, core: 2. Of those that a mesh axis runs over, the one named last changes fastest.
Arguments:
- descriptors: bfloat16 [16384, 2048], P('atoms', 'pivots'), may hold values from -6 to 6
- pivot_desc: bfloat16 [32768, 2048], P('pivots'), may hold values from -6 to 6
- coeffs: float32 [32768, 64], P('pivots'), may hold values from -0.00390625 to 0.00390625
- seg_ids: int32 [16, 1024], P('atoms'), may hold values from 0 to 127, never falling along the last dimension, each value on 1 to 24 neighbouring positions
- dest: int32 [2048], replicated, may hold values from 0 to 2047, as said below
- targets: float32 [2048, 64], P('atoms'), may hold values from -6 to 6
- weights: float32 [2048], P('atoms'), may hold values from 0.5 to 2
Outputs:
- residual: float32 [2048, 64], P('atoms', 'pivots')
- gradient: float32 [64, 32768], P('atoms', 'pivots')
Inputs may be any that keep to these rules, and one draw needn't show every extreme that they name: dest is a permutation; the structures of home a (indices a * 128 to a * 128 + 127) go to owners dest // 128; at most 32 structures of one home go to one owner, some home sends exactly 32 to one owner, and every owner receives exactly 128. `seg_ids`: row a numbers the structure of each atom of home a; numbers never fall along a row and every number appears.
All inputs are finite; a program needn't handle non-finite values.
Results may differ from a plain program's by a relative error of at most 0.0011.
Values may be sent and summed in bfloat16 or wider, within the bound.
A program may use at most 64 MiB of HBM per device.

v0:
```python
import jax
import jax.numpy as jnp
from jax import lax
from jax.sharding import PartitionSpec as P

eps = 1e-06


def row_scale(matrix):
    squares = jnp.sum(jnp.square(matrix.astype(jnp.float32)), axis=1)
    return lax.rsqrt(squares + eps)


def select_rows(table, values):
    return jnp.dot(
        table, values, precision=lax.Precision.HIGHEST, preferred_element_type=jnp.float32
    )


def spread(table, values):
    return lax.dot_general(
        table,
        values,
        (((0,), (0,)), ((), ())),
        precision=lax.Precision.HIGHEST,
        preferred_element_type=jnp.float32,
    )


def routing(destination, struct_dev, capacity, shard_count, myself):
    struct_total = shard_count * struct_dev
    owner_all = destination // struct_dev
    owner_grid = owner_all.reshape(shard_count, struct_dev)
    one_hot = (
        owner_grid[:, :, None] == jnp.arange(shard_count, dtype=jnp.int32)[None, None, :]
    ).astype(jnp.int32)
    earlier = jnp.cumsum(one_hot, axis=1) - one_hot
    ranking = jnp.sum(earlier * one_hot, axis=2).reshape(struct_total)
    home_all = jnp.arange(struct_total, dtype=jnp.int32) // struct_dev
    arrival_row = home_all * capacity + ranking
    first_own = myself * struct_dev
    owner_mine = lax.dynamic_slice_in_dim(owner_all, first_own, struct_dev)
    rank_mine = lax.dynamic_slice_in_dim(ranking, first_own, struct_dev)
    send_rows = owner_mine * capacity + rank_mine
    slot_index = jnp.arange(shard_count * capacity, dtype=jnp.int32)
    home_pick = (send_rows[:, None] == slot_index[None, :]).astype(jnp.float32)
    wanted = first_own + jnp.arange(struct_dev, dtype=jnp.int32)
    matches = destination[None, :] == wanted[:, None]
    row_of_position = jnp.sum(jnp.where(matches, arrival_row[None, :], 0), axis=1)
    owner_pick = (row_of_position[:, None] == slot_index[None, :]).astype(jnp.float32)
    return (home_pick, owner_pick)


def on_device(descriptors, pivot_desc, coeffs, seg_ids, dest, targets, weights):
    pivot_scale = row_scale(pivot_desc)
    desc_width = pivot_desc.shape[1]
    full_atoms = lax.all_gather(descriptors, "pivots", axis=1, tiled=True)
    scores = lax.dot_general(
        full_atoms, pivot_desc, (((1,), (1,)), ((), ())), preferred_element_type=jnp.float32
    )
    atom_scale = row_scale(full_atoms)
    cosine = scores * atom_scale[:, None] * pivot_scale[None, :]
    kernel_tile = (desc_width * jnp.square(cosine)).astype(jnp.bfloat16)
    struct_dev = targets.shape[0]
    members = (seg_ids[0][None, :] == jnp.arange(struct_dev, dtype=jnp.int32)[:, None]).astype(
        jnp.bfloat16
    )
    structure_kernel = jnp.dot(members, kernel_tile, preferred_element_type=jnp.float32)
    partial_predicted = jnp.dot(
        structure_kernel,
        coeffs,
        precision=lax.Precision.HIGHEST,
        preferred_element_type=jnp.float32,
    )
    shard_count = lax.axis_size("atoms")
    myself = lax.axis_index("atoms")
    capacity = struct_dev // 4
    home_pick, owner_pick = routing(dest, struct_dev, capacity, shard_count, myself)
    n_targets = targets.shape[1]
    column_share = n_targets // lax.axis_size("pivots")
    first_column = lax.axis_index("pivots") * column_share
    predicted = lax.psum(partial_predicted, "pivots")
    owner_weights = weights[:, None]
    outgoing = spread(home_pick, predicted)
    arrived_rows = lax.all_to_all(outgoing, "atoms", split_axis=0, concat_axis=0, tiled=True)
    at_owner = select_rows(owner_pick, arrived_rows)
    owner_residual = owner_weights * (at_owner - targets)
    returned = lax.all_to_all(
        spread(owner_pick, owner_residual), "atoms", split_axis=0, concat_axis=0, tiled=True
    )
    residual = select_rows(home_pick, returned)
    residual_out = lax.dynamic_slice_in_dim(residual, first_column, column_share, 1)
    struct_total = struct_dev * shard_count
    term = lax.dot_general(
        residual,
        structure_kernel,
        (((0,), (0,)), ((), ())),
        precision=lax.Precision.HIGHEST,
        preferred_element_type=jnp.float32,
    )
    gradient = lax.psum_scatter(term / struct_total, "atoms", scatter_dimension=0, tiled=True)
    return (residual_out, gradient)


def solution(mesh):
    placed = (
        P("atoms", "pivots"),
        P("pivots", None),
        P("pivots", None),
        P("atoms", None),
        P(),
        P("atoms", None),
        P("atoms"),
    )
    return jax.shard_map(
        on_device,
        mesh=mesh,
        in_specs=placed,
        out_specs=(P("atoms", "pivots"), P("atoms", "pivots")),
        check_vma=False,
    )
```

profile of v0, /device:TPU:2, one launch (start us, length us, event | category | flops | bytes accessed | tf_op | source)
XLA Modules:
  0.0 398.0 jit_solution(11424266951960315301)
XLA Ops:
  7.2 0.0 copy-start
  7.2 0.0 all-gather.2.cloned.1.call-start
  7.2 0.7 all-gather.2.cloned.1.call-update
  7.9 0.7 add_select_fusion.1
  8.6 0.1 copy.19
  8.7 2.8 select_reduce_fusion.1
  11.5 0.1 copy.20
  11.6 0.1 dynamic-slice_add_fusion
  11.6 0.0 copy-start.4
  11.7 3.1 multiply_reduce_fusion
  14.8 61.9 %all-gather.2.cloned.1.call-done = bf16[1024,2048]{0,1:T(8,128)(2,1)} async-done(((bf16[1024,64]{0,1:T(8,128)(2,1)}), bf16[1024,2048]{0,1:T(8,128)(2,1)}) %all-gather.2.cloned.1.call-update) | async-done | bytes 4194320 | tf_op jit(solution)/shard_map/all_gather | solution.py:57
  76.6 3.1 multiply_reduce_fusion.1
  79.8 0.0 copy-done.4
  79.8 0.0 copy-start.2
  79.8 0.0 copy-start.1
  79.8 0.0 copy-start.3
  79.8 8.8 %fusion.4 = f32[128,1024]{1,0:T(8,128)S(1)} fusion(bf16[1024,2048]{0,1:T(8,128)(2,1)} %all-gather.2.cloned.1.call-done, bf16[1024,2048]{1,0:T(8,128)(2,1)} %param.8, f32[1024]{0:T(1024)S(1)} %add_rsqrt_fusion, f32[1024]{0:T(1024)S(1)} %add_rsqrt_fusion.1, s32[1024]{0:T(1024)S(1)} %bitcast.25), kind=kOutput, calls=%fused_computation.6 | convolution fusion | flops 4568776704 | bytes 8925184 | tf_op jit(solution)/shard_map/dot_general | solution.py:68
  88.6 0.0 copy-done
  88.6 0.7 fusion.28
  89.3 121.5 %psum.7 = f32[128,64]{0,1:T(8,128)S(1)} all-reduce(f32[128,64]{0,1:T(8,128)S(1)} %fusion.28), channel_id=1, replica_groups=mesh['atoms'=16,'pivots'=32] {'pivots'}, use_global_device_ids=true, to_apply=%region_5.6 | all-reduce | flops 8192 | bytes 65536 | tf_op jit(solution)/shard_map/psum | solution.py:82
  210.8 0.4 fusion.11
  211.2 0.8 reshape.49
  212.0 12.3 %all-to-all-start = ((f32[16,1,2048]{2,1,0:T(1,128)}), f32[16,1,2048]{2,1,0:T(1,128)S(1)}, u32[]{:S(2)}, u32[]{:S(2)}) async-start(f32[16,1,2048]{2,1,0:T(1,128)} %reshape.49), calls=%async_computation | async-start | bytes 262144 | tf_op jit(solution)/shard_map/all_to_all | solution.py:85
  224.3 0.2 all-reduce.3.cloned.1.call-start
  224.6 0.0 copy-done.2
  224.6 0.2 select_reduce_fusion
  224.8 12.6 %all-to-all-done = f32[16,1,2048]{2,1,0:T(1,128)S(1)} async-done(((f32[16,1,2048]{2,1,0:T(1,128)}), f32[16,1,2048]{2,1,0:T(1,128)S(1)}, u32[]{:S(2)}, u32[]{:S(2)}) %all-to-all-start) | async-done | bytes 131104 | tf_op jit(solution)/shard_map/all_to_all | solution.py:85
  237.4 0.5 broadcast.73
  237.9 1.0 reduce
  238.9 0.1 reshape.50
  239.0 0.0 copy-done.1
  239.0 0.0 copy-done.3
  239.0 0.4 fusion.5
  239.4 0.4 fusion.13
  239.8 0.2 reshape.51
  240.0 17.1 %all_to_all.24 = f32[16,1,2048]{2,1,0:T(1,128)S(1)} all-to-all(f32[16,1,2048]{2,1,0:T(1,128)S(1)} %reshape.51), channel_id=1, replica_groups=mesh['atoms'=16,'pivots'=32] {'atoms'}, dimensions={0} | all-to-all | bytes 262144 | tf_op jit(solution)/shard_map/all_to_all | solution.py:88
  257.1 1.0 reduce.1
  258.0 0.1 reshape.52
  258.2 0.4 fusion.9
  258.6 1.1 convolution_multiply_fusion
  259.7 0.0 all-reduce.3.cloned.1.call-update
  259.7 1.3 dynamic-slice
  261.7 0.6 constant_dynamic-slice_fusion.1
  262.2 127.5 %all-reduce.3.cloned.1.call-done = f32[64,1024]{1,0:T(8,128)} async-done(((f32[64,1024]{1,0:T(8,128)}), f32[64,1024]{1,0:T(8,128)}) %all-reduce.3.cloned.1.call-update) | async-done | bytes 262160
  389.7 1.4 constant_dynamic-slice_fusion
  (4 shorter events, 0.0 us)
Async XLA Ops:
  7.2 81.4 %copy-start = (f32[1024,64]{0,1:T(8,128)S(1)}, f32[1024,64]{0,1:T(8,128)}, u32[]{:S(2)}) copy-start(f32[1024,64]{0,1:T(8,128)} %param.9) | copy-start | bytes 786436
  7.2 69.5 %all-gather.2.cloned.1.call-start = ((), (), s32[]{:S(2)}) async-start(), calls=%async_computation.2 | async-start | bytes 4325376 | tf_op jit(solution)/shard_map/all_gather | solution.py:57
  11.6 68.1 %copy-start.4 = (s32[1,1024]{1,0:T(1,128)S(1)}, s32[1,1024]{1,0:T(1,128)}, u32[]{:S(2)}) copy-start(s32[1,1024]{1,0:T(1,128)} %param.10) | copy-start | bytes 12292
  79.8 144.8 %copy-start.2 = (s32[2048]{0:T(1024)S(1)}, s32[2048]{0:T(1024)}, u32[]{:S(2)}) copy-start(s32[2048]{0:T(1024)} %param.11) | copy-start | bytes 24580
  79.8 159.2 %copy-start.1 = (f32[128,64]{0,1:T(8,128)S(1)}, f32[128,64]{0,1:T(8,128)}, u32[]{:S(2)}) copy-start(f32[128,64]{0,1:T(8,128)} %param.12) | copy-start | bytes 98308
  79.8 159.2 %copy-start.3 = (f32[128]{0:T(128)S(1)}, f32[128]{0:T(128)}, u32[]{:S(2)}) copy-start(f32[128]{0:T(128)} %param.13) | copy-start | bytes 1540
  212.0 25.4 %all-to-all-start = ((f32[16,1,2048]{2,1,0:T(1,128)}), f32[16,1,2048]{2,1,0:T(1,128)S(1)}, u32[]{:S(2)}, u32[]{:S(2)}) async-start(f32[16,1,2048]{2,1,0:T(1,128)} %reshape.49), calls=%async_computation | async-start | bytes 262144 | tf_op jit(solution)/shard_map/all_to_all | solution.py:85
  224.3 165.4 %all-reduce.3.cloned.1.call-start = ((), (), s32[]{:S(2)}) async-start(), calls=%async_computation.3 | async-start | bytes 524288
Sparse Core Ops, SparseCore 0:
  11.1 65.4 all-gather.1
  259.8 129.8 all-reduce.2
where the time goes:
time: 398 us
  waiting for transfers between devices  203 us (51%)
  blocking collectives  139 us (35%)
  between operations  14.9 us (4%)
  starting transfers between devices  12.5 us (3%)
  matrix products  12.2 us (3%)
  other arithmetic  12 us (3%)
  local copies, waits for them, and re-layouts  5.11 us (1%)
    unnamed x3, waiting for transfers between devices  128 us
    psum x1, blocking collectives, on_device(): predicted = lax.psum(partial_predicted, 'pivots')  122 us
    all_gather x1, waiting for transfers between devices, on_device(): full_atoms = lax.all_gather(descriptors, 'pivots', axis=1, tiled=True)  61.9 us
    all_to_all x1, blocking collectives, on_device(): lax.all_to_all(spread(owner_pick, owner_residual), 'atoms', split_axis=0,...  17.1 us
    all_to_all x1, waiting for transfers between devices, on_device(): lax.all_to_all(outgoing, 'atoms', split_axis=0, concat_axis=0, tiled=True)  12.6 us
    all_to_all x1, starting transfers between devices, on_device(): lax.all_to_all(outgoing, 'atoms', split_axis=0, concat_axis=0, tiled=True)  12.3 us
    dot_general x1, matrix products, on_device(): jnp.dot(members, kernel_tile, preferred_element_type=jnp.float32)  8.79 us
  transfers between devices with their start and end apart: 3, of which 3 were waited for; matrix products, arithmetic and copies ran while one was open for 2% of the time, Pallas kernels for 0%

commit v1 on v0

v1 whole, which is shorter than its diff:
```python
import functools

import jax
import jax.numpy as jnp
from jax import lax
from jax.experimental import pallas as pl
from jax.experimental.pallas import tpu as pltpu
from jax.sharding import PartitionSpec as P

EPS = 1e-6
MESH = pl.DeviceIdType.MESH
F32 = jnp.float32
BF16 = jnp.bfloat16
NB = 4
NZ = 16
NX = 4


def split2(value):
    high = value.astype(BF16)
    low = (value - high.astype(F32)).astype(BF16)
    return high, low


def split3(value):
    high = value.astype(BF16)
    rest = value - high.astype(F32)
    mid = rest.astype(BF16)
    low = (rest - mid.astype(F32)).astype(BF16)
    return high, mid, low


def mm(left, right):
    return jnp.dot(left, right, preferred_element_type=F32)


def kernel(
    d_ref,
    p_ref,
    c_ref,
    seg_ref,
    dest_ref,
    tgt_ref,
    w_ref,
    res_ref,
    grad_ref,
    gathered,
    pv,
    cv,
    segv,
    destv,
    tgtv,
    wv,
    p2,
    members,
    skt,
    sht,
    slt,
    tz,
    pred_send,
    pred_recv,
    tiles,
    grad_send,
    grad_recv,
    arow,
    local_sem,
    own_sem,
    line_sem,
    half_sem,
    part_send_sem,
    recv_sem,
    part_recv_sem,
    z_send_sem,
    z_recv_sem,
    late_sem,
):
    z = lax.axis_index("atoms")
    p = lax.axis_index("pivots")
    c = lax.rem(p, 2)
    x = lax.rem(lax.div(p, 2), NX)
    y = lax.div(p, 2 * NX)
    q = lax.div(p, 4)
    rows = d_ref.shape[0]
    half = rows // 2
    atoms = d_ref.shape[1]
    width = atoms // NB
    pivots = p_ref.shape[0]
    tile = pivots // 4
    structs = tz.shape[2]

    def wrap(value):
        return lax.rem(value + NX, NX)

    def place(f, s):
        return wrap(y + s * (1 - c) + f * c), wrap(x + f * (1 - c) + s * c)

    def device(f, s):
        yi, xi = place(f, s)
        return (z, (yi * NX + xi) * 2 + c)

    partner = (z, p + 1 - 2 * c)
    up = (lax.rem(z + 1, NZ), p)
    down = (lax.rem(z + NZ - 1, NZ), p)
    f_up, f_down = device(1, 0), device(-1, 0)
    s_up, s_down = device(0, 1), device(0, -1)

    locals_ = [
        pltpu.make_async_copy(tgt_ref, tgtv, local_sem.at[0]),
        pltpu.make_async_copy(w_ref, wv, local_sem.at[1]),
        pltpu.make_async_copy(seg_ref, segv, local_sem.at[2]),
        pltpu.make_async_copy(p_ref, pv, local_sem.at[3]),
        pltpu.make_async_copy(c_ref, cv, local_sem.at[4]),
        pltpu.make_async_copy(dest_ref, destv, local_sem.at[5]),
        pltpu.make_async_copy(d_ref, gathered.at[y, x, c], local_sem.at[6]),
    ]
    barrier = pltpu.get_barrier_semaphore()
    for peer in (f_up, f_down, s_up, s_down, partner, up, down):
        pl.semaphore_signal(barrier, inc=1, device_id=peer, device_id_type=MESH)
    for copy in locals_:
        copy.start()
    pl.semaphore_wait(barrier, 7)

    def span(b):
        return pl.ds(pl.multiple_of(b * width, width), width)

    def own(b):
        for kind, peer in ((0, f_up), (1, f_down), (2, s_up), (3, s_down)):
            pltpu.make_async_remote_copy(
                src_ref=d_ref.at[:, span(b)],
                dst_ref=gathered.at[y, x, c, :, span(b)],
                send_sem=own_sem,
                recv_sem=recv_sem.at[kind, b],
                device_id=peer,
                device_id_type=MESH,
            ).start()
        pltpu.make_async_remote_copy(
            src_ref=d_ref.at[:, span(b)],
            dst_ref=gathered.at[y, x, c, :, span(b)],
            send_sem=part_send_sem,
            recv_sem=part_recv_sem.at[b],
            device_id=partner,
            device_id_type=MESH,
        ).start()

    for b in range(NB):
        own(b)

    def piece(spot, part, b):
        yi, xi = spot
        return gathered.at[yi, xi, c, part, span(b)]

    whole, low, high = pl.ds(0, rows), pl.ds(0, half), pl.ds(half, half)

    def forward(kind, b, spot, part, sem, peer):
        ref = piece(spot, part, b)
        pltpu.make_async_remote_copy(
            src_ref=ref,
            dst_ref=ref,
            send_sem=sem,
            recv_sem=recv_sem.at[kind, b],
            device_id=peer,
            device_id_type=MESH,
        ).start()

    def share(b, spot):
        ref = piece(spot, whole, b)
        pltpu.make_async_remote_copy(
            src_ref=ref,
            dst_ref=ref,
            send_sem=part_send_sem,
            recv_sem=part_recv_sem.at[b],
            device_id=partner,
            device_id_type=MESH,
        ).start()

    def arrive(kind, b, spot, part):
        ref = piece(spot, part, b)
        pltpu.make_async_remote_copy(
            src_ref=ref,
            dst_ref=ref,
            send_sem=own_sem,
            recv_sem=recv_sem.at[kind, b],
            device_id=partner,
            device_id_type=MESH,
        ).wait_recv()

    to_low, to_high = half_sem.at[0], half_sem.at[1]

    def event1(b):
        spot = place(-1, 0)
        arrive(0, b, spot, whole)
        forward(4, b, spot, low, to_low, f_up)
        forward(6, b, spot, whole, line_sem, s_up)
        forward(7, b, spot, whole, line_sem, s_down)
        share(b, spot)
        spot = place(1, 0)
        arrive(1, b, spot, whole)
        forward(5, b, spot, high, to_low, f_down)
        forward(8, b, spot, whole, line_sem, s_up)
        forward(9, b, spot, whole, line_sem, s_down)
        share(b, spot)
        spot = place(0, -1)
        arrive(2, b, spot, whole)
        forward(12, b, spot, low, to_high, s_up)
        share(b, spot)
        spot = place(0, 1)
        arrive(3, b, spot, whole)
        forward(13, b, spot, high, to_high, s_down)
        share(b, spot)

    def event2(b):
        spot = place(2, 0)
        arrive(4, b, spot, low)
        arrive(5, b, spot, high)
        forward(10, b, spot, whole, line_sem, s_up)
        forward(11, b, spot, whole, line_sem, s_down)
        share(b, spot)
        for f, first in ((-1, 6), (1, 8)):
            spot = place(f, -1)
            arrive(first, b, spot, whole)
            forward(first + 8, b, spot, low, to_high, s_up)
            share(b, spot)
            spot = place(f, 1)
            arrive(first + 1, b, spot, whole)
            forward(first + 9, b, spot, high, to_high, s_down)
            share(b, spot)
        spot = place(0, 2)
        arrive(12, b, spot, low)
        arrive(13, b, spot, high)
        share(b, spot)

    def event3(b):
        spot = place(2, -1)
        arrive(10, b, spot, whole)
        forward(18, b, spot, low, to_high, s_up)
        share(b, spot)
        spot = place(2, 1)
        arrive(11, b, spot, whole)
        forward(19, b, spot, high, to_high, s_down)
        share(b, spot)
        for f, first in ((-1, 14), (1, 16)):
            spot = place(f, 2)
            arrive(first, b, spot, low)
            arrive(first + 1, b, spot, high)
            share(b, spot)

    def event4(b):
        spot = place(2, 2)
        arrive(18, b, spot, low)
        arrive(19, b, spot, high)
        share(b, spot)

    def event5(b):
        ref = gathered.at[:, :, 1 - c, :, span(b)]
        pltpu.make_async_remote_copy(
            src_ref=ref,
            dst_ref=ref,
            send_sem=own_sem,
            recv_sem=part_recv_sem.at[b],
            device_id=partner,
            device_id_type=MESH,
        ).wait_recv()

    def ring(slot, step, way):
        ref = tz.at[slot]
        return pltpu.make_async_remote_copy(
            src_ref=ref,
            dst_ref=ref,
            send_sem=z_send_sem.at[step, way],
            recv_sem=z_recv_sem.at[step, way],
            device_id=up if way == 0 else down,
            device_id_type=MESH,
        )

    locals_[0].wait()
    locals_[1].wait()
    tz[z, 0:8, :] = tgtv[q]
    tz[z, 8:16, :] = jnp.broadcast_to(wv[...], (8, structs))
    ring(z, 0, 0).start()
    ring(z, 0, 1).start()

    locals_[2].wait()
    ids = lax.broadcasted_iota(jnp.int32, (structs, atoms), 0)
    chosen = jnp.where(ids == segv[...], 1.0, 0.0).astype(F32)
    members[...] = chosen.T.astype(BF16)
    skt[...] = jnp.zeros_like(skt)
    locals_[6].wait()
    locals_[3].wait()

    def pivot_scales(k):
        at = pl.ds(pl.multiple_of(k * tile, tile), tile)
        total = jnp.zeros((tile, 128), F32)
        for j in range(pv.shape[1] // 128):
            part = pv[at, j * 128 : (j + 1) * 128].astype(F32)
            total = total + part * part
        scale = lax.rsqrt(jnp.sum(total, axis=1, keepdims=True) + EPS)
        squared = (desc_width * scale) * scale
        p2[at, :] = jnp.broadcast_to(squared, (tile, 128))

    desc_width = float(pv.shape[1])

    def atom_row(b):
        total = jnp.zeros((8, width), F32)
        for yi in range(NX):
            for xi in range(NX):
                part = gathered[yi, xi, :, :, span(b)].astype(F32)
                part = (part * part).reshape(2 * rows // 8, 8, width)
                total = total + jnp.sum(part, axis=0)
        arow[...] = lax.rsqrt(jnp.sum(total, axis=0, keepdims=True) + EPS)

    def compute(b, j):
        at = pl.ds(j * tile, tile)
        right = gathered[:, :, :, :, span(b)].reshape(pv.shape[1], width)
        scores = mm(pv[at, :], right)
        scaled = scores * arow[...]
        scaled = scaled * scaled
        factor = p2[at, :]
        factor = jnp.concatenate([factor] * (width // 128), axis=1)
        entries = (scaled * factor).astype(BF16)
        skt[at, :] += mm(entries, members[span(b), :])

    def step(k, carry):
        done = k - 4

        @pl.when(done >= 0)
        def _():
            event5(done)
            atom_row(done)

        stages = ((event4, 3), (event3, 2), (event2, 1), (event1, 0))
        for j, (event, lag) in enumerate(stages):

            @pl.when(jnp.logical_and(k >= lag, k < NB + lag))
            def _(event=event, lag=lag):
                event(k - lag)

            @pl.when(done >= 0)
            def _(j=j):
                compute(done, j)

        slot = lax.rem(z + NZ - 1 - k, NZ)
        ring(slot, k, 0).wait_recv()

        @pl.when(k < 7)
        def _():
            ring(slot, k + 1, 0).start()
            other = lax.rem(z + 1 + k, NZ)
            ring(other, k, 1).wait_recv()

            @pl.when(k < 6)
            def _():
                ring(other, k + 1, 1).start()

        @pl.when(k < 4)
        def _():
            pivot_scales(k)

        return carry

    lax.fori_loop(0, 8, step, 0)

    locals_[4].wait()
    coef_high, coef_low = split2(cv[...])
    sk_high, sk_low = split2(skt[...])
    n_targets = cv.shape[0]
    first = mm(jnp.concatenate([coef_high, coef_low], axis=0), sk_high)
    predicted = first[:n_targets] + first[n_targets:] + mm(coef_high, sk_low)
    pred_send[...] = predicted.reshape(n_targets // 8, 8, structs)
    pred_recv[p] = pred_send[q]

    def exchange(src_slot, dst_slot, peer):
        return pltpu.make_async_remote_copy(
            src_ref=pred_send.at[src_slot],
            dst_ref=pred_recv.at[dst_slot],
            send_sem=late_sem.at[0],
            recv_sem=late_sem.at[1],
            device_id=peer,
            device_id_type=MESH,
        )

    n_plane = pred_recv.shape[0]

    def send_tile(i, carry):
        peer = lax.rem(p + i, n_plane)
        exchange(lax.div(peer, 4), p, (z, peer)).start()
        return carry

    lax.fori_loop(1, n_plane, send_tile, 0)

    locals_[5].wait()
    wanted = destv[pl.ds(z, 1), :]
    home = jnp.zeros((48, structs), F32)
    for owner in range(NZ):
        spots = lax.broadcasted_iota(jnp.int32, (structs, structs), 0) + owner * structs
        pick = jnp.where(spots == wanted, 1.0, 0.0).astype(BF16)
        home = home + mm(jnp.concatenate(split3(tz[owner]), axis=0), pick)
    home = (home[0:16] + home[16:32]) + home[32:48]
    turned = skt[...].T
    sk_high, sk_low = split2(turned)
    sht[...] = sk_high
    slt[...] = sk_low

    def settle(ref, sem, sending):
        copy = pltpu.make_async_remote_copy(
            src_ref=ref,
            dst_ref=ref,
            send_sem=sem,
            recv_sem=sem,
            device_id=partner,
            device_id_type=MESH,
        )
        if sending:
            copy.wait_send()
        else:
            copy.wait_recv()

    settle(pred_recv.at[pl.ds(0, n_plane - 1)], late_sem.at[1], False)
    summed = jnp.sum(pred_recv[...], axis=0)
    resid = home[8:16] * (summed - home[0:8])
    tiles[q] = resid

    def tile_copy(yi, xi):
        return pltpu.make_async_remote_copy(
            src_ref=tiles.at[q],
            dst_ref=tiles.at[q],
            send_sem=late_sem.at[2],
            recv_sem=late_sem.at[3],
            device_id=(z, (yi * NX + xi) * 2 + c),
            device_id_type=MESH,
        )

    for dy in (2, 1, 3, 0):
        yi = lax.rem(y + dy, NX)
        tile_copy(yi, NX - 1 - x).start()
        if dy:
            tile_copy(yi, x).start()
    mine = lax.rem(p, 4)
    out = resid[0:2]
    for j in range(1, 4):
        out = jnp.where(mine == j, resid[2 * j : 2 * j + 2], out)
    res_ref[...] = out
    settle(tiles.at[pl.ds(0, 7)], late_sem.at[3], False)

    res_high, res_low = split2(tiles[...].reshape(n_targets, structs))
    first = mm(jnp.concatenate([res_high, res_low], axis=0), sht[...])
    grads = first[:n_targets] + first[n_targets:] + mm(res_high, slt[...])
    grads = grads * (1.0 / (structs * NZ))
    share_rows = n_targets // NZ
    for owner in range(NZ):
        grad_send[owner] = grads[owner * share_rows : (owner + 1) * share_rows]
    grad_recv[z] = grad_send[z]

    def send_grad(i, carry):
        peer = lax.rem(z + i, NZ)
        pltpu.make_async_remote_copy(
            src_ref=grad_send.at[peer],
            dst_ref=grad_recv.at[z],
            send_sem=late_sem.at[4],
            recv_sem=late_sem.at[5],
            device_id=(peer, p),
            device_id_type=MESH,
        ).start()
        return carry

    lax.fori_loop(1, NZ, send_grad, 0)

    settle(gathered.at[0, :, c], own_sem, True)
    settle(gathered.at[0:2, 0:3, c], line_sem, True)
    settle(gathered.at[0, 0, c], half_sem.at[0], True)
    settle(gathered.at[0, :, c], half_sem.at[1], True)
    settle(gathered.at[:, :, c], part_send_sem, True)
    for k in range(8):
        ring(z, k, 0).wait_send()
        if k < 7:
            ring(z, k, 1).wait_send()
    settle(pred_recv.at[pl.ds(0, n_plane - 1)], late_sem.at[0], True)
    settle(tiles.at[pl.ds(0, 7)], late_sem.at[2], True)
    settle(grad_recv.at[pl.ds(0, NZ - 1)], late_sem.at[5], False)
    grad_ref[...] = jnp.sum(grad_recv[...], axis=0)
    settle(grad_send.at[pl.ds(0, NZ - 1)], late_sem.at[4], True)


def on_device(descriptors, pivot_desc, coeffs, seg_ids, dest, targets, weights):
    atoms, rows = descriptors.shape
    pivots, width = pivot_desc.shape
    structs, n_targets = targets.shape
    any_spec = pl.BlockSpec(memory_space=pltpu.HBM)
    vmem_spec = pl.BlockSpec(memory_space=pltpu.VMEM)
    dma = pltpu.SemaphoreType.DMA
    res, grad = pl.pallas_call(
        kernel,
        out_shape=(
            jax.ShapeDtypeStruct((n_targets // 32, structs), F32),
            jax.ShapeDtypeStruct((n_targets // NZ, pivots), F32),
        ),
        in_specs=[any_spec] * 7,
        out_specs=(vmem_spec, vmem_spec),
        scratch_shapes=[
            pltpu.VMEM((NX, NX, 2, rows, atoms), BF16),
            pltpu.VMEM((pivots, width), BF16),
            pltpu.VMEM((n_targets, pivots), F32),
            pltpu.VMEM((1, atoms), jnp.int32),
            pltpu.VMEM((NZ, structs), jnp.int32),
            pltpu.VMEM((n_targets // 8, 8, structs), F32),
            pltpu.VMEM((1, structs), F32),
            pltpu.VMEM((pivots, 128), F32),
            pltpu.VMEM((atoms, structs), BF16),
            pltpu.VMEM((pivots, structs), F32),
            pltpu.VMEM((structs, pivots), BF16),
            pltpu.VMEM((structs, pivots), BF16),
            pltpu.VMEM((NZ, 16, structs), F32),
            pltpu.VMEM((n_targets // 8, 8, structs), F32),
            pltpu.VMEM((32, 8, structs), F32),
            pltpu.VMEM((n_targets // 8, 8, structs), F32),
            pltpu.VMEM((NZ, n_targets // NZ, pivots), F32),
            pltpu.VMEM((NZ, n_targets // NZ, pivots), F32),
            pltpu.VMEM((1, atoms // NB), F32),
            dma((7,)),
            dma,
            dma,
            dma((2,)),
            dma,
            dma((20, NB)),
            dma((NB,)),
            dma((8, 2)),
            dma((8, 2)),
            dma((6,)),
        ],
        compiler_params=pltpu.CompilerParams(
            collective_id=0, has_side_effects=True, vmem_limit_bytes=60 * 1024 * 1024
        ),
        name="fit_gradient",
    )(
        descriptors.T,
        pivot_desc,
        coeffs.T,
        seg_ids,
        dest.reshape(NZ, structs),
        targets.T.reshape(n_targets // 8, 8, structs),
        weights.reshape(1, structs),
    )
    return res.T, grad


def solution(mesh):
    placed = (
        P("atoms", "pivots"),
        P("pivots", None),
        P("pivots", None),
        P("atoms", None),
        P(),
        P("atoms", None),
        P("atoms"),
    )
    return jax.shard_map(
        on_device,
        mesh=mesh,
        in_specs=placed,
        out_specs=(P("atoms", "pivots"), P("atoms", "pivots")),
        check_vma=False,
    )
```

time: 398 us -> 76.3 us (0.19)
  the two profiles are of different devices: /device:TPU:2 before, /device:TPU:8 now
where the time goes in v1:
time: 76.3 us; the launch traced here: 76 us
  Pallas kernels  72.8 us (95%)
  local copies, waits for them, and re-layouts  2.54 us (3%)
    pallas_call x1, Pallas kernels, on_device(): pl.pallas_call(kernel, out_shape=(jax.ShapeDtypeStruct((n_targets // 32,...  72.8 us
    unnamed x2, local copies, waits for them, and re-layouts  2.54 us

profile of v1, /device:TPU:8, one launch (start us, length us, event | category | flops | bytes accessed | tf_op | source)
XLA Modules:
  0.0 76.0 jit_solution(499135331566644927)
XLA Ops:
  0.6 72.8 %fit_gradient.1 = (f32[2,128]{1,0:T(2,128)}, f32[4,1024]{1,0:T(4,128)}) custom-call(bf16[64,1024]{1,0:T(8,128)(2,1)} %bitcast.9, bf16[1024,2048]{1,0:T(8,128)(2,1)} %p_ref.1, f32[64,1024]{1,0:T(8,128)} %bitcast.8, s32[1,1024]{1,0:T(1,128)} %seg_ref.1, s32[16,128]{1,0:T(8,128)} %bitcast.11, f32[8,8,128]{2,1,0:T(8,128)} %bitcast.10, f32[1,128]{1,0:T(1,128)} %bitcast.13), custom_call_target="tpu_custom_call" | custom-call | tf_op jit(solution)/shard_map/fit_gradient/pallas_call | solution.py:490
  73.5 1.2 %copy.11 = f32[128,2]{0,1:T(2,128)} copy(f32[128,2]{0,1:T(2,128)} %bitcast.12) | data formatting | bytes 2048
  74.7 1.3 %copy.12 = f32[4,1024]{1,0:T(4,128)} copy(f32[4,1024]{1,0:T(4,128)} %get-tuple-element.9) | data formatting | bytes 32768

commit v2 on v1

--- a/solution.py
+++ b/solution.py
@@ -11,7 +11,8 @@
 MESH = pl.DeviceIdType.MESH
 F32 = jnp.float32
 BF16 = jnp.bfloat16
-NB = 4
+CODES = 32766.0
+NB = 2
 NZ = 16
 NX = 4
 
@@ -62,7 +63,10 @@
     tiles,
     grad_send,
     grad_recv,
-    arow,
+    step_send,
+    step_recv,
+    squares,
+    scores,
     local_sem,
     own_sem,
     line_sem,
@@ -70,8 +74,7 @@
     part_send_sem,
     recv_sem,
     part_recv_sem,
-    z_send_sem,
-    z_recv_sem,
+    known_sem,
     late_sem,
 ):
     z = lax.axis_index("atoms")
@@ -137,7 +140,7 @@
             src_ref=d_ref.at[:, span(b)],
             dst_ref=gathered.at[y, x, c, :, span(b)],
             send_sem=part_send_sem,
-            recv_sem=part_recv_sem.at[b],
+            recv_sem=part_recv_sem.at[0],
             device_id=partner,
             device_id_type=MESH,
         ).start()
@@ -162,13 +165,13 @@
             device_id_type=MESH,
         ).start()
 
-    def share(b, spot):
+    def share(b, spot, group):
         ref = piece(spot, whole, b)
         pltpu.make_async_remote_copy(
             src_ref=ref,
             dst_ref=ref,
             send_sem=part_send_sem,
-            recv_sem=part_recv_sem.at[b],
+            recv_sem=part_recv_sem.at[group],
             device_id=partner,
             device_id_type=MESH,
         ).start()
@@ -192,21 +195,21 @@
         forward(4, b, spot, low, to_low, f_up)
         forward(6, b, spot, whole, line_sem, s_up)
         forward(7, b, spot, whole, line_sem, s_down)
-        share(b, spot)
+        share(b, spot, 1)
         spot = place(1, 0)
         arrive(1, b, spot, whole)
         forward(5, b, spot, high, to_low, f_down)
         forward(8, b, spot, whole, line_sem, s_up)
         forward(9, b, spot, whole, line_sem, s_down)
-        share(b, spot)
+        share(b, spot, 1)
         spot = place(0, -1)
         arrive(2, b, spot, whole)
         forward(12, b, spot, low, to_high, s_up)
-        share(b, spot)
+        share(b, spot, 1)
         spot = place(0, 1)
         arrive(3, b, spot, whole)
         forward(13, b, spot, high, to_high, s_down)
-        share(b, spot)
+        share(b, spot, 1)
 
     def event2(b):
         spot = place(2, 0)
@@ -214,76 +217,67 @@
         arrive(5, b, spot, high)
         forward(10, b, spot, whole, line_sem, s_up)
         forward(11, b, spot, whole, line_sem, s_down)
-        share(b, spot)
+        share(b, spot, 2)
         for f, first in ((-1, 6), (1, 8)):
             spot = place(f, -1)
             arrive(first, b, spot, whole)
             forward(first + 8, b, spot, low, to_high, s_up)
-            share(b, spot)
+            share(b, spot, 2)
             spot = place(f, 1)
             arrive(first + 1, b, spot, whole)
             forward(first + 9, b, spot, high, to_high, s_down)
-            share(b, spot)
+            share(b, spot, 2)
         spot = place(0, 2)
         arrive(12, b, spot, low)
         arrive(13, b, spot, high)
-        share(b, spot)
+        share(b, spot, 2)
 
     def event3(b):
         spot = place(2, -1)
         arrive(10, b, spot, whole)
         forward(18, b, spot, low, to_high, s_up)
-        share(b, spot)
+        share(b, spot, 3)
         spot = place(2, 1)
         arrive(11, b, spot, whole)
         forward(19, b, spot, high, to_high, s_down)
-        share(b, spot)
+        share(b, spot, 3)
         for f, first in ((-1, 14), (1, 16)):
             spot = place(f, 2)
             arrive(first, b, spot, low)
             arrive(first + 1, b, spot, high)
-            share(b, spot)
+            share(b, spot, 3)
 
     def event4(b):
         spot = place(2, 2)
         arrive(18, b, spot, low)
         arrive(19, b, spot, high)
-        share(b, spot)
-
-    def event5(b):
-        ref = gathered.at[:, :, 1 - c, :, span(b)]
+        share(b, spot, 4)
+
+    def shared(ref, group):
         pltpu.make_async_remote_copy(
             src_ref=ref,
             dst_ref=ref,
             send_sem=own_sem,
-            recv_sem=part_recv_sem.at[b],
+            recv_sem=part_recv_sem.at[group],
             device_id=partner,
             device_id_type=MESH,
         ).wait_recv()
 
-    def ring(slot, step, way):
-        ref = tz.at[slot]
-        return pltpu.make_async_remote_copy(
-            src_ref=ref,
-            dst_ref=ref,
-            send_sem=z_send_sem.at[step, way],
-            recv_sem=z_recv_sem.at[step, way],
-            device_id=up if way == 0 else down,
-            device_id_type=MESH,
-        )
+    def greet(distance, step):
+        for peer in (lax.rem(z + distance, NZ), lax.rem(z + NZ - distance, NZ)):
+            pl.semaphore_signal(known_sem.at[step], inc=1, device_id=(peer, p), device_id_type=MESH)
+
+    greet(1, 0)
 
     locals_[0].wait()
     locals_[1].wait()
     tz[z, 0:8, :] = tgtv[q]
     tz[z, 8:16, :] = jnp.broadcast_to(wv[...], (8, structs))
-    ring(z, 0, 0).start()
-    ring(z, 0, 1).start()
 
     locals_[2].wait()
     ids = lax.broadcasted_iota(jnp.int32, (structs, atoms), 0)
     chosen = jnp.where(ids == segv[...], 1.0, 0.0).astype(F32)
     members[...] = chosen.T.astype(BF16)
-    skt[...] = jnp.zeros_like(skt)
     locals_[6].wait()
     locals_[3].wait()
 
@@ -299,65 +293,99 @@
 
     desc_width = float(pv.shape[1])
 
-    def atom_row(b):
-        total = jnp.zeros((8, width), F32)
-        for yi in range(NX):
-            for xi in range(NX):
-                part = gathered[yi, xi, :, :, span(b)].astype(F32)
-                part = (part * part).reshape(2 * rows // 8, 8, width)
-                total = total + jnp.sum(part, axis=0)
-        arow[...] = lax.rsqrt(jnp.sum(total, axis=0, keepdims=True) + EPS)
-
-    def compute(b, j):
-        at = pl.ds(j * tile, tile)
-        right = gathered[:, :, :, :, span(b)].reshape(pv.shape[1], width)
-        scores = mm(pv[at, :], right)
-        scaled = scores * arow[...]
-        scaled = scaled * scaled
-        factor = p2[at, :]
-        factor = jnp.concatenate([factor] * (width // 128), axis=1)
-        entries = (scaled * factor).astype(BF16)
-        skt[at, :] += mm(entries, members[span(b), :])
-
-    def step(k, carry):
-        done = k - 4
-
-        @pl.when(done >= 0)
-        def _():
-            event5(done)
-            atom_row(done)
-
-        stages = ((event4, 3), (event3, 2), (event2, 1), (event1, 0))
-        for j, (event, lag) in enumerate(stages):
-
-            @pl.when(jnp.logical_and(k >= lag, k < NB + lag))
-            def _(event=event, lag=lag):
-                event(k - lag)
-
-            @pl.when(done >= 0)
-            def _(j=j):
-                compute(done, j)
-
-        slot = lax.rem(z + NZ - 1 - k, NZ)
-        ring(slot, k, 0).wait_recv()
-
-        @pl.when(k < 7)
-        def _():
-            ring(slot, k + 1, 0).start()
-            other = lax.rem(z + 1 + k, NZ)
-            ring(other, k, 1).wait_recv()
-
-            @pl.when(k < 6)
-            def _():
-                ring(other, k + 1, 1).start()
-
-        @pl.when(k < 4)
-        def _():
-            pivot_scales(k)
-
-        return carry
-
-    lax.fori_loop(0, 8, step, 0)
+    def chip(dy, dx):
+        return wrap(y + dy), wrap(x + dx)
+
+    def operand(chips):
+        parts = [gathered[yi, xi].reshape(2 * rows, atoms) for yi, xi in chips]
+        return jnp.concatenate(parts, axis=0)
+
+    def columns(at, chips):
+        parts = []
+        for yi, xi in chips:
+            first = pl.multiple_of((yi * NX + xi) * 2 * rows, 128)
+            parts.append(pv[at, pl.ds(first, 2 * rows)])
+        return jnp.concatenate(parts, axis=1)
+
+    def add_squares(chips, start):
+        total = jnp.zeros((8, atoms), F32) if start else squares[...]
+        for yi, xi in chips:
+            part = gathered[yi, xi].astype(F32)
+            part = (part * part).reshape(2 * rows // 8, 8, atoms)
+            total = total + jnp.sum(part, axis=0)
+        squares[...] = total
+
+    def add_scores(chips, start):
+        right = operand(chips)
+        for j in range(pivots // tile):
+            at = pl.ds(j * tile, tile)
+            part = mm(columns(at, chips), right)
+            scores[at, :] = part if start else scores[at, :] + part
+        add_squares(chips, start)
+
+    def finish(chips):
+        add_squares(chips, False)
+        row = lax.rsqrt(jnp.sum(squares[...], axis=0, keepdims=True) + EPS)
+        right = operand(chips)
+        for j in range(pivots // tile):
+            at = pl.ds(j * tile, tile)
+            scaled = (scores[at, :] + mm(columns(at, chips), right)) * row
+            scaled = scaled * scaled
+            factor = jnp.concatenate([p2[at, :]] * (atoms // 128), axis=1)
+            entries = (scaled * factor).astype(BF16)
+            skt[at, :] = mm(entries, members[...])
+
+    def settle(ref, sem, sending):
+        copy = pltpu.make_async_remote_copy(
+            src_ref=ref,
+            dst_ref=ref,
+            send_sem=sem,
+            recv_sem=sem,
+            device_id=partner,
+            device_id_type=MESH,
+        )
+        if sending:
+            copy.wait_send()
+        else:
+            copy.wait_recv()
+
+    def send_owner(i):
+        pltpu.make_async_remote_copy(
+            src_ref=tz.at[z],
+            dst_ref=tz.at[z],
+            send_sem=late_sem.at[8],
+            recv_sem=late_sem.at[9],
+            device_id=(lax.rem(z + i, NZ), p),
+            device_id_type=MESH,
+        ).start()
+
+    event1(0)
+    pl.semaphore_wait(known_sem.at[0], 2)
+    greet(2, 1)
+    for b in range(1, NB):
+        event1(b)
+    for k in range(pivots // tile):
+        pivot_scales(k)
+    pl.semaphore_wait(known_sem.at[1], 2)
+    greet(4, 2)
+    shared(gathered.at[0, :, c], 1)
+    add_scores([chip(0, -1), chip(0, 1), chip(-1, 0), chip(1, 0)], True)
+    for b in range(NB):
+        event2(b)
+    pl.semaphore_wait(known_sem.at[2], 2)
+    for i in (8, 7, 9, 6, 10, 5, 11, 4, 12, 3, 13, 2, 14, 1, 15):
+        send_owner(i)
+    shared(gathered.at[0, 0, c], 0)
+    shared(gathered.at[0:2, 0:3, c], 2)
+    add_scores([chip(0, 0), chip(0, 2), chip(-1, -1), chip(-1, 1), chip(1, -1), chip(1, 1)], False)
+    for b in range(NB):
+        event3(b)
+    shared(gathered.at[0, :, c], 3)
+    add_scores([chip(2, 0), chip(1, 2), chip(-1, 2), chip(2, -1)], False)
+    for b in range(NB):
+        event4(b)
+    shared(gathered.at[0, 0, c], 4)
+    finish([chip(2, 1), chip(2, 2)])
 
     locals_[4].wait()
     coef_high, coef_low = split2(cv[...])
@@ -380,14 +408,14 @@
 
     n_plane = pred_recv.shape[0]
 
-    def send_tile(i, carry):
-        peer = lax.rem(p + i, n_plane)
+    far = sorted(range(1, n_plane), key=lambda i: -sum(min(v, NX - v) for v in (i // 2 // NX, i // 2 % NX)))
+    for i in far:
+        yi, xi = chip(i // 2 // NX, i // 2 % NX)
+        peer = (yi * NX + xi) * 2 + (c if i % 2 == 0 else 1 - c)
         exchange(lax.div(peer, 4), p, (z, peer)).start()
-        return carry
-
-    lax.fori_loop(1, n_plane, send_tile, 0)
 
     locals_[5].wait()
+    settle(tz.at[pl.ds(0, NZ - 1)], late_sem.at[9], False)
     wanted = destv[pl.ds(z, 1), :]
     home = jnp.zeros((48, structs), F32)
     for owner in range(NZ):
@@ -400,20 +428,6 @@
     sht[...] = sk_high
     slt[...] = sk_low
 
-    def settle(ref, sem, sending):
-        copy = pltpu.make_async_remote_copy(
-            src_ref=ref,
-            dst_ref=ref,
-            send_sem=sem,
-            recv_sem=sem,
-            device_id=partner,
-            device_id_type=MESH,
-        )
-        if sending:
-            copy.wait_send()
-        else:
-            copy.wait_recv()
-
     settle(pred_recv.at[pl.ds(0, n_plane - 1)], late_sem.at[1], False)
     summed = jnp.sum(pred_recv[...], axis=0)
     resid = home[8:16] * (summed - home[0:8])
@@ -446,37 +460,56 @@
     grads = first[:n_targets] + first[n_targets:] + mm(res_high, slt[...])
     grads = grads * (1.0 / (structs * NZ))
     share_rows = n_targets // NZ
+    largest = jnp.max(jnp.max(jnp.abs(grads), axis=0, keepdims=True), axis=1, keepdims=True)
+    largest = jnp.maximum(jnp.broadcast_to(largest, (1, 128)), 1e-30)
+    step_send[...] = largest * (1.0 / CODES)
+    to_code = jnp.broadcast_to(CODES / largest, (n_targets, 128))
+    to_code = jnp.concatenate([to_code] * (pivots // 128), axis=1)
+    codes = jnp.floor(grads * to_code + 0.5).astype(jnp.int32)
     for owner in range(NZ):
-        grad_send[owner] = grads[owner * share_rows : (owner + 1) * share_rows]
+        part = codes[owner * share_rows : (owner + 1) * share_rows]
+        part = jnp.concatenate([part[:, k * 256 : (k + 1) * 256] for k in range(pivots // 256)], axis=0)
+        grad_send[owner] = part.astype(jnp.int16)
     grad_recv[z] = grad_send[z]
+    step_recv[z] = step_send[...]
 
     def send_grad(i, carry):
         peer = lax.rem(z + i, NZ)
-        pltpu.make_async_remote_copy(
-            src_ref=grad_send.at[peer],
-            dst_ref=grad_recv.at[z],
-            send_sem=late_sem.at[4],
-            recv_sem=late_sem.at[5],
-            device_id=(peer, p),
-            device_id_type=MESH,
-        ).start()
+        for src, dst, sem in (
+            (grad_send.at[peer], grad_recv.at[z], 4),
+            (step_send, step_recv.at[z], 6),
+        ):
+            pltpu.make_async_remote_copy(
+                src_ref=src,
+                dst_ref=dst,
+                send_sem=late_sem.at[sem],
+                recv_sem=late_sem.at[sem + 1],
+                device_id=(peer, p),
+                device_id_type=MESH,
+            ).start()
         return carry
 
-    lax.fori_loop(1, NZ, send_grad, 0)
+    for i in (8, 7, 9, 6, 10, 5, 11, 4, 12, 3, 13, 2, 14, 1, 15):
+        send_grad(i, 0)
 
     settle(gathered.at[0, :, c], own_sem, True)
     settle(gathered.at[0:2, 0:3, c], line_sem, True)
     settle(gathered.at[0, 0, c], half_sem.at[0], True)
     settle(gathered.at[0, :, c], half_sem.at[1], True)
     settle(gathered.at[:, :, c], part_send_sem, True)
-    for k in range(8):
-        ring(z, k, 0).wait_send()
-        if k < 7:
-            ring(z, k, 1).wait_send()
+    settle(tz.at[pl.ds(0, NZ - 1)], late_sem.at[8], True)
     settle(pred_recv.at[pl.ds(0, n_plane - 1)], late_sem.at[0], True)
     settle(tiles.at[pl.ds(0, 7)], late_sem.at[2], True)
     settle(grad_recv.at[pl.ds(0, NZ - 1)], late_sem.at[5], False)
-    grad_ref[...] = jnp.sum(grad_recv[...], axis=0)
+    settle(step_recv.at[pl.ds(0, NZ - 1)], late_sem.at[7], False)
+    settle(step_recv.at[pl.ds(0, NZ - 1)], late_sem.at[6], True)
+    total = jnp.zeros(grad_recv.shape[1:], F32)
+    for src in range(NZ):
+        scale = step_recv[src]
+        scale = jnp.concatenate([scale, scale], axis=1)
+        total = total + grad_recv[src].astype(jnp.int32).astype(F32) * scale
+    for k in range(pivots // 256):
+        grad_ref[:, k * 256 : (k + 1) * 256] = total[k * share_rows : (k + 1) * share_rows]
     settle(grad_send.at[pl.ds(0, NZ - 1)], late_sem.at[4], True)
 
 
@@ -512,19 +545,21 @@
             pltpu.VMEM((n_targets // 8, 8, structs), F32),
             pltpu.VMEM((32, 8, structs), F32),
             pltpu.VMEM((n_targets // 8, 8, structs), F32),
-            pltpu.VMEM((NZ, n_targets // NZ, pivots), F32),
-            pltpu.VMEM((NZ, n_targets // NZ, pivots), F32),
-            pltpu.VMEM((1, atoms // NB), F32),
+            pltpu.VMEM((NZ, 16, 256), jnp.int16),
+            pltpu.VMEM((NZ, 16, 256), jnp.int16),
+            pltpu.VMEM((1, 128), F32),
+            pltpu.VMEM((NZ, 1, 128), F32),
+            pltpu.VMEM((8, atoms), F32),
+            pltpu.VMEM((pivots, atoms), F32),
             dma((7,)),
             dma,
             dma,
             dma((2,)),
             dma,
             dma((20, NB)),
-            dma((NB,)),
-            dma((8, 2)),
-            dma((8, 2)),
-            dma((6,)),
+            dma((5,)),
+            pltpu.SemaphoreType.REGULAR((3,)),
+            dma((10,)),
         ],
         compiler_params=pltpu.CompilerParams(
             collective_id=0, has_side_effects=True, vmem_limit_bytes=60 * 1024 * 1024

time: 76.3 us -> 55 us (0.72)
  Pallas kernels: 72.8 us -> 51.6 us
    pallas_call x1, Pallas kernels: 72.8 us -> 51.6 us  [on_device(): pl.pallas_call(kernel, out_shape=(jax.ShapeDtypeStruct((n_targets // 32,...]
where the time goes in v2:
time: 55 us; the launch traced here: 54.7 us
  Pallas kernels  51.6 us (94%)
  local copies, waits for them, and re-layouts  2.54 us (5%)
  between operations  0.64 us (1%)
    pallas_call x1, Pallas kernels, on_device(): pl.pallas_call(kernel, out_shape=(jax.ShapeDtypeStruct((n_targets // 32,...  51.6 us
    unnamed x2, local copies, waits for them, and re-layouts  2.54 us

profile of v2, /device:TPU:8, one launch (start us, length us, event | category | flops | bytes accessed | tf_op | source)
XLA Modules:
  0.0 54.7 jit_solution(5930013194895673188)
XLA Ops:
  0.6 51.6 %fit_gradient.1 = (f32[2,128]{1,0:T(2,128)}, f32[4,1024]{1,0:T(4,128)}) custom-call(bf16[64,1024]{1,0:T(8,128)(2,1)} %bitcast.9, bf16[1024,2048]{1,0:T(8,128)(2,1)} %p_ref.1, f32[64,1024]{1,0:T(8,128)} %bitcast.8, s32[1,1024]{1,0:T(1,128)} %seg_ref.1, s32[16,128]{1,0:T(8,128)} %bitcast.11, f32[8,8,128]{2,1,0:T(8,128)} %bitcast.10, f32[1,128]{1,0:T(1,128)} %bitcast.13), custom_call_target="tpu_custom_call" | custom-call | tf_op jit(solution)/shard_map/fit_gradient/pallas_call | solution.py:523
  52.2 1.2 %copy.11 = f32[128,2]{0,1:T(2,128)} copy(f32[128,2]{0,1:T(2,128)} %bitcast.12) | data formatting | bytes 2048
  53.4 1.3 %copy.12 = f32[4,1024]{1,0:T(4,128)} copy(f32[4,1024]{1,0:T(4,128)} %get-tuple-element.9) | data formatting | bytes 32768

commit v3 on v2

--- a/solution.py
+++ b/solution.py
@@ -119,8 +119,9 @@
     barrier = pltpu.get_barrier_semaphore()
     for peer in (f_up, f_down, s_up, s_down, partner, up, down):
         pl.semaphore_signal(barrier, inc=1, device_id=peer, device_id_type=MESH)
-    for copy in locals_:
-        copy.start()
+    locals_[6].start()
+    for k in (0, 1, 2):
+        locals_[k].start()
     pl.semaphore_wait(barrier, 7)
 
     def span(b):
@@ -129,7 +130,7 @@
     def own(b):
         for kind, peer in ((0, f_up), (1, f_down), (2, s_up), (3, s_down)):
             pltpu.make_async_remote_copy(
-                src_ref=d_ref.at[:, span(b)],
+                src_ref=gathered.at[y, x, c, :, span(b)],
                 dst_ref=gathered.at[y, x, c, :, span(b)],
                 send_sem=own_sem,
                 recv_sem=recv_sem.at[kind, b],
@@ -137,7 +138,7 @@
                 device_id_type=MESH,
             ).start()
         pltpu.make_async_remote_copy(
-            src_ref=d_ref.at[:, span(b)],
+            src_ref=gathered.at[y, x, c, :, span(b)],
             dst_ref=gathered.at[y, x, c, :, span(b)],
             send_sem=part_send_sem,
             recv_sem=part_recv_sem.at[0],
@@ -145,8 +146,11 @@
             device_id_type=MESH,
         ).start()
 
+    locals_[6].wait()
     for b in range(NB):
         own(b)
+    for k in (3, 4, 5):
+        locals_[k].start()
 
     def piece(spot, part, b):
         yi, xi = spot
@@ -278,8 +282,6 @@
     ids = lax.broadcasted_iota(jnp.int32, (structs, atoms), 0)
     chosen = jnp.where(ids == segv[...], 1.0, 0.0).astype(F32)
     members[...] = chosen.T.astype(BF16)
-    locals_[6].wait()
-    locals_[3].wait()
 
     def pivot_scales(k):
         at = pl.ds(pl.multiple_of(k * tile, tile), tile)
@@ -359,31 +361,31 @@
             device_id_type=MESH,
         ).start()
 
+    locals_[3].wait()
+    for k in range(pivots // tile):
+        pivot_scales(k)
     event1(0)
     pl.semaphore_wait(known_sem.at[0], 2)
     greet(2, 1)
-    for b in range(1, NB):
-        event1(b)
-    for k in range(pivots // tile):
-        pivot_scales(k)
+    event1(1)
     pl.semaphore_wait(known_sem.at[1], 2)
     greet(4, 2)
-    shared(gathered.at[0, :, c], 1)
-    add_scores([chip(0, -1), chip(0, 1), chip(-1, 0), chip(1, 0)], True)
-    for b in range(NB):
-        event2(b)
+    event2(0)
+    event2(1)
     pl.semaphore_wait(known_sem.at[2], 2)
     for i in (8, 7, 9, 6, 10, 5, 11, 4, 12, 3, 13, 2, 14, 1, 15):
         send_owner(i)
+    shared(gathered.at[0, :, c], 1)
+    add_scores([chip(0, -1), chip(0, 1), chip(-1, 0), chip(1, 0)], True)
+    event3(0)
+    event3(1)
     shared(gathered.at[0, 0, c], 0)
     shared(gathered.at[0:2, 0:3, c], 2)
     add_scores([chip(0, 0), chip(0, 2), chip(-1, -1), chip(-1, 1), chip(1, -1), chip(1, 1)], False)
-    for b in range(NB):
-        event3(b)
+    event4(0)
+    event4(1)
     shared(gathered.at[0, :, c], 3)
     add_scores([chip(2, 0), chip(1, 2), chip(-1, 2), chip(2, -1)], False)
-    for b in range(NB):
-        event4(b)
     shared(gathered.at[0, 0, c], 4)
     finish([chip(2, 1), chip(2, 2)])
 
@@ -462,10 +464,11 @@
     share_rows = n_targets // NZ
     largest = jnp.max(jnp.max(jnp.abs(grads), axis=0, keepdims=True), axis=1, keepdims=True)
     largest = jnp.maximum(jnp.broadcast_to(largest, (1, 128)), 1e-30)
-    step_send[...] = largest * (1.0 / CODES)
-    to_code = jnp.broadcast_to(CODES / largest, (n_targets, 128))
-    to_code = jnp.concatenate([to_code] * (pivots // 128), axis=1)
-    codes = jnp.floor(grads * to_code + 0.5).astype(jnp.int32)
+    step_send[...] = largest * (1.0 / CODES**2)
+    to_one = jnp.broadcast_to(1.0 / largest, (n_targets, 128))
+    to_one = jnp.concatenate([to_one] * (pivots // 128), axis=1)
+    codes = jnp.floor(jnp.sqrt(jnp.abs(grads) * to_one) * CODES + 0.5)
+    codes = jnp.where(grads < 0, -codes, codes).astype(jnp.int32)
     for owner in range(NZ):
         part = codes[owner * share_rows : (owner + 1) * share_rows]
         part = jnp.concatenate([part[:, k * 256 : (k + 1) * 256] for k in range(pivots // 256)], axis=0)
@@ -507,7 +510,8 @@
     for src in range(NZ):
         scale = step_recv[src]
         scale = jnp.concatenate([scale, scale], axis=1)
-        total = total + grad_recv[src].astype(jnp.int32).astype(F32) * scale
+        code = grad_recv[src].astype(jnp.int32).astype(F32)
+        total = total + (code * jnp.abs(code)) * scale
     for k in range(pivots // 256):
         grad_ref[:, k * 256 : (k + 1) * 256] = total[k * share_rows : (k + 1) * share_rows]
     settle(grad_send.at[pl.ds(0, NZ - 1)], late_sem.at[4], True)
@@ -523,8 +527,8 @@
     res, grad = pl.pallas_call(
         kernel,
         out_shape=(
-            jax.ShapeDtypeStruct((n_targets // 32, structs), F32),
-            jax.ShapeDtypeStruct((n_targets // NZ, pivots), F32),
+            pltpu.VMEM((n_targets // 32, structs), F32),
+            pltpu.VMEM((n_targets // NZ, pivots), F32),
         ),
         in_specs=[any_spec] * 7,
         out_specs=(vmem_spec, vmem_spec),

time: 55 us -> 52.4 us (0.953)
  local copies, waits for them, and re-layouts: 2.54 us -> 1.17 us
  Pallas kernels: 51.6 us -> 50.5 us
    unnamed x2, local copies, waits for them, and re-layouts: 2.54 us -> 1.17 us
    pallas_call x1, Pallas kernels: 51.6 us -> 50.5 us  [on_device(): pl.pallas_call(kernel, out_shape=(pltpu.VMEM((n_targets // 32, structs),...]
where the time goes in v3:
time: 52.4 us; the launch traced here: 52.3 us
  Pallas kernels  50.5 us (96%)
  local copies, waits for them, and re-layouts  1.17 us (2%)
  between operations  0.64 us (1%)
    pallas_call x1, Pallas kernels, on_device(): pl.pallas_call(kernel, out_shape=(pltpu.VMEM((n_targets // 32, structs),...  50.5 us
    unnamed x2, local copies, waits for them, and re-layouts  1.17 us

profile of v3, /device:TPU:8, one launch (start us, length us, event | category | flops | bytes accessed | tf_op | source)
XLA Modules:
  0.0 52.3 jit_solution(4102444630786143188)
XLA Ops:
  0.6 50.5 %fit_gradient.1 = (f32[2,128]{1,0:T(2,128)S(1)}, f32[4,1024]{1,0:T(4,128)S(1)}) custom-call(bf16[64,1024]{1,0:T(8,128)(2,1)} %bitcast.10, bf16[1024,2048]{1,0:T(8,128)(2,1)} %p_ref.1, f32[64,1024]{1,0:T(8,128)} %bitcast.9, s32[1,1024]{1,0:T(1,128)} %seg_ref.1, s32[16,128]{1,0:T(8,128)} %bitcast.12, f32[8,8,128]{2,1,0:T(8,128)} %bitcast.11, f32[1,128]{1,0:T(1,128)} %bitcast.13), custom_call_target="tpu_custom_call" | custom-call | tf_op jit(solution)/shard_map/fit_gradient/pallas_call | solution.py:527
  51.1 0.6 %copy.11 = f32[128,2]{0,1:T(2,128)} copy(f32[128,2]{0,1:T(2,128)S(1)} %bitcast.8) | data formatting | bytes 2048
  51.7 0.6 %copy.12 = f32[4,1024]{1,0:T(4,128)} copy(f32[4,1024]{1,0:T(4,128)S(1)} %get-tuple-element.7) | data formatting | bytes 32768

commit v4 on v3

--- a/solution.py
+++ b/solution.py
@@ -515,6 +515,17 @@
     for k in range(pivots // 256):
         grad_ref[:, k * 256 : (k + 1) * 256] = total[k * share_rows : (k + 1) * share_rows]
     settle(grad_send.at[pl.ds(0, NZ - 1)], late_sem.at[4], True)
+
+
+def store(res_ref, grad_ref, res_out, grad_out, sem):
+    copies = [
+        pltpu.make_async_copy(res_ref, res_out, sem.at[0]),
+        pltpu.make_async_copy(grad_ref, grad_out, sem.at[1]),
+    ]
+    for copy in copies:
+        copy.start()
+    for copy in copies:
+        copy.wait()
 
 
 def on_device(descriptors, pivot_desc, coeffs, seg_ids, dest, targets, weights):
@@ -578,6 +589,20 @@
         targets.T.reshape(n_targets // 8, 8, structs),
         weights.reshape(1, structs),
     )
+    res, grad = pl.pallas_call(
+        store,
+        out_shape=(
+            jax.ShapeDtypeStruct(res.shape, F32),
+            jax.ShapeDtypeStruct(grad.shape, F32),
+        ),
+        in_specs=[vmem_spec, vmem_spec],
+        out_specs=(any_spec, any_spec),
+        scratch_shapes=[dma((2,))],
+        name="store_results",
+    )(
+        pltpu.with_memory_space_constraint(res, pltpu.VMEM),
+        pltpu.with_memory_space_constraint(grad, pltpu.VMEM),
+    )
     return res.T, grad
 
 

time: 52.4 us -> 51.9 us (level)
  local copies, waits for them, and re-layouts: 1.17 us -> 0 us
  Pallas kernels: 50.5 us -> 51.1 us
    unnamed x2 -> x0, local copies, waits for them, and re-layouts: 1.17 us -> none
    pallas_call x0 -> x1, Pallas kernels: none -> 0.63 us  [on_device(): pl.pallas_call(store, out_shape=(jax.ShapeDtypeStruct(res.shape, F32), ja...]
where the time goes in v4:
time: 51.9 us; the launch traced here: 51.8 us
  Pallas kernels  51.1 us (98%)
  between operations  0.64 us (1%)
    pallas_call x1, Pallas kernels, on_device(): pl.pallas_call(kernel, out_shape=(pltpu.VMEM((n_targets // 32, structs),...  50.5 us

profile of v4, /device:TPU:8, one launch (start us, length us, event | category | flops | bytes accessed | tf_op | source)
XLA Modules:
  0.0 51.8 jit_solution(18322431703374849751)
XLA Ops:
  0.6 50.5 %fit_gradient.1 = (f32[2,128]{1,0:T(2,128)S(1)}, f32[4,1024]{1,0:T(4,128)S(1)}) custom-call(bf16[64,1024]{1,0:T(8,128)(2,1)} %bitcast.9, bf16[1024,2048]{1,0:T(8,128)(2,1)} %p_ref.1, f32[64,1024]{1,0:T(8,128)} %bitcast.8, s32[1,1024]{1,0:T(1,128)} %seg_ref.1, s32[16,128]{1,0:T(8,128)} %bitcast.11, f32[8,8,128]{2,1,0:T(8,128)} %bitcast.10, f32[1,128]{1,0:T(1,128)} %bitcast.12), custom_call_target="tpu_custom_call" | custom-call | tf_op jit(solution)/shard_map/fit_gradient/pallas_call | solution.py:538
  51.1 0.6 %store_results.1 = (f32[2,128]{1,0:T(2,128)}, f32[4,1024]{1,0:T(4,128)}) custom-call(f32[2,128]{1,0:T(2,128)S(1)} %get-tuple-element.6.res_ref, f32[4,1024]{1,0:T(4,128)S(1)} %get-tuple-element.7.grad_ref), custom_call_target="tpu_custom_call" | custom-call | tf_op jit(solution)/shard_map/store_results/pallas_call | solution.py:592

commit v5 on v4

--- a/solution.py
+++ b/solution.py
@@ -194,18 +194,17 @@
     to_low, to_high = half_sem.at[0], half_sem.at[1]
 
     def event1(b):
-        spot = place(-1, 0)
-        arrive(0, b, spot, whole)
-        forward(4, b, spot, low, to_low, f_up)
-        forward(6, b, spot, whole, line_sem, s_up)
-        forward(7, b, spot, whole, line_sem, s_down)
-        share(b, spot, 1)
-        spot = place(1, 0)
-        arrive(1, b, spot, whole)
-        forward(5, b, spot, high, to_low, f_down)
-        forward(8, b, spot, whole, line_sem, s_up)
-        forward(9, b, spot, whole, line_sem, s_down)
-        share(b, spot, 1)
+        before, after = place(-1, 0), place(1, 0)
+        arrive(0, b, before, whole)
+        forward(4, b, before, low, to_low, f_up)
+        arrive(1, b, after, whole)
+        forward(5, b, after, high, to_low, f_down)
+        forward(6, b, before, whole, line_sem, s_up)
+        forward(7, b, before, whole, line_sem, s_down)
+        forward(8, b, after, whole, line_sem, s_up)
+        forward(9, b, after, whole, line_sem, s_down)
+        share(b, before, 1)
+        share(b, after, 1)
         spot = place(0, -1)
         arrive(2, b, spot, whole)
         forward(12, b, spot, low, to_high, s_up)

time: 51.9 us -> 51.9 us (level)
  no operation moved by 1% of the time
where the time goes in v5:
time: 51.9 us; the launch traced here: 51.8 us
  Pallas kernels  51.1 us (98%)
  between operations  0.64 us (1%)
    pallas_call x1, Pallas kernels, on_device(): pl.pallas_call(kernel, out_shape=(pltpu.VMEM((n_targets // 32, structs),...  50.5 us

profile of v5, /device:TPU:8, one launch (start us, length us, event | category | flops | bytes accessed | tf_op | source)
XLA Modules:
  0.0 51.8 jit_solution(9354515676345463843)
XLA Ops:
  0.6 50.5 %fit_gradient.1 = (f32[2,128]{1,0:T(2,128)S(1)}, f32[4,1024]{1,0:T(4,128)S(1)}) custom-call(bf16[64,1024]{1,0:T(8,128)(2,1)} %bitcast.9, bf16[1024,2048]{1,0:T(8,128)(2,1)} %p_ref.1, f32[64,1024]{1,0:T(8,128)} %bitcast.8, s32[1,1024]{1,0:T(1,128)} %seg_ref.1, s32[16,128]{1,0:T(8,128)} %bitcast.11, f32[8,8,128]{2,1,0:T(8,128)} %bitcast.10, f32[1,128]{1,0:T(1,128)} %bitcast.12), custom_call_target="tpu_custom_call" | custom-call | tf_op jit(solution)/shard_map/fit_gradient/pallas_call | solution.py:537
  51.1 0.6 %store_results.1 = (f32[2,128]{1,0:T(2,128)}, f32[4,1024]{1,0:T(4,128)}) custom-call(f32[2,128]{1,0:T(2,128)S(1)} %get-tuple-element.6.res_ref, f32[4,1024]{1,0:T(4,128)S(1)} %get-tuple-element.7.grad_ref), custom_call_target="tpu_custom_call" | custom-call | tf_op jit(solution)/shard_map/store_results/pallas_call | solution.py:591
